TPU v7x, 32 devices: a whole 2x2x4 slice. The times are simulated.
32 devices in a mesh: dp: 2 (over x), row: 4 (over z), col: 4 (over y, core).
Axes of the slice: x: 2, y: 2, z: 4, core: 2. Of those that a mesh axis runs over, the one named last changes fastest.
Arguments:
- tokens: bfloat16 [16, 768, 1024], P(('dp', 'row'), 'col'), may hold values from -6 to 6
- memory: bfloat16 [16, 20, 768], P(('dp', 'row'), None, 'col'), may hold values from -6 to 6
- block_ids: int32 [16, 1024], P(('dp', 'row')), may hold values from 0 to 7, never falling along the last dimension, each value on 1 to 256 neighbouring positions
- valid: int32 [16], replicated, may hold values from 512 to 1024
- teacher: bfloat16 [16, 768, 1024], P(('dp', 'row'), 'col'), may hold values from -6 to 6
- w_qkv: bfloat16 [12, 147456], P('row', 'col'), may hold values from -0.21875 to 0.21875
- bias_qv: float32 [12, 128], P('row'), may hold values from -3 to 3
- w_out: bfloat16 [768, 768], P('row', 'col'), may hold values from -0.875 to 0.875
- bias_out: float32 [768], P('col'), may hold values from -2 to 2
- ln1_gain: float32 [768], P('col'), may hold values from 0.1 to 1.9
- ln1_bias: float32 [768], P('col'), may hold values from -2 to 2
- w_up: bfloat16 [768, 3072], P('col', 'row'), may hold values from -0.21875 to 0.21875
- bias_up: float32 [3072], P('row'), may hold values from -3 to 3
- w_down: bfloat16 [768, 3072], P('col', 'row'), may hold values from -0.109375 to 0.109375
- bias_down: float32 [768], P('col'), may hold values from -2 to 2
- ln2_gain: float32 [768], P('col'), may hold values from 0.1 to 1.9
- ln2_bias: float32 [768], P('col'), may hold values from -2 to 2
Outputs:
- layer_out: bfloat16 [16, 1044, 768], P(('dp', 'row'), None, 'col')
- grad_tokens: float32 [16, 1024, 768], P(('dp', 'row'), None, 'col')
- grad_memory: float32 [16, 20, 768], P(('dp', 'row'), None, 'col')
- grad_w_qkv: float32 [12, 147456], P('row', 'col')
- grad_bias_qv: float32 [12, 128], P('row')
- grad_w_out: float32 [768, 768], P('row', 'col')
- grad_bias_out: float32 [768], P('col')
- grad_ln1_gain: float32 [768], P('col')
- grad_ln1_bias: float32 [768], P('col')
- grad_w_up: float32 [768, 3072], P('col', 'row')
- grad_bias_up: float32 [3072], P('row')
- grad_w_down: float32 [768, 3072], P('col', 'row')
- grad_bias_down: float32 [768], P('col')
- grad_ln2_gain: float32 [768], P('col')
- grad_ln2_bias: float32 [768], P('col')
Inputs may be any that keep to these rules, and one draw needn't show every extreme that they name: `block_ids`: along each sequence the numbers never fall; each of the 8 numbers covers 1 to 256 consecutive tokens.
All inputs are finite; a program needn't handle non-finite values.
Results may differ from a plain program's by a relative error of at most 0.015.
Values may be sent and summed in bfloat16 or wider, within the bound.
A program may use at most 192 MiB of HBM per device.

v0:
```python
from functools import partial
import jax
import jax.numpy as jnp
from jax import lax
from jax.sharding import PartitionSpec as P

EPSILON = 1e-12
NEGATIVE = -1e30


def gather_feats(shard):
    return lax.all_gather(shard, "col", axis=1, tiled=True)


def back_gather(shard):
    return lax.all_gather(shard, "col", axis=1, tiled=True)


def forward_reduce(partial_rows):
    return lax.psum_scatter(
        partial_rows.astype(jnp.bfloat16), "col", scatter_dimension=1, tiled=True
    ).astype(jnp.float32)


def backward_reduce(partial_rows):
    return lax.psum_scatter(
        partial_rows.astype(jnp.bfloat16), "col", scatter_dimension=1, tiled=True
    ).astype(jnp.float32)


def against(piece_rows, matrix):
    return lax.dot_general(
        piece_rows, matrix, (((1,), (1,)), ((), ())), preferred_element_type=jnp.float32
    )


def column_total(piece_rows):
    unit_row = jnp.ones((1, piece_rows.shape[0]), jnp.bfloat16)
    return jnp.dot(unit_row, piece_rows, preferred_element_type=jnp.float32)[0]


def outer_sum(left_rows, right_rows):
    return lax.dot_general(
        left_rows, right_rows, (((0,), (0,)), ((), ())), preferred_element_type=jnp.float32
    )


def assemble(stacked, row_size, col_size):
    shape = stacked.shape
    grid = stacked.reshape((row_size, col_size) + shape[1:])
    moved = jnp.swapaxes(grid, 1, 2)
    return moved.reshape((row_size * shape[1], col_size * shape[2]) + shape[3:])


def norm_forward(summed, gain, shift, feat_total):
    sum_plain, sum_square = lax.psum(
        (jnp.sum(summed, axis=1), jnp.sum(summed * summed, axis=1)), "col"
    )
    average = sum_plain / feat_total
    inverse = lax.rsqrt(sum_square / feat_total - average * average + EPSILON)
    scaled = (summed - average[:, None]) * inverse[:, None]
    return (scaled * gain + shift, scaled, inverse)


def norm_backward(cotangent, scaled, inverse, gain, feat_total):
    weighted = cotangent * gain
    sum_plain, sum_cross = lax.psum(
        (jnp.sum(weighted, axis=1), jnp.sum(weighted * scaled, axis=1)), "col"
    )
    inner = weighted - sum_plain[:, None] / feat_total - scaled * (sum_cross[:, None] / feat_total)
    return (
        inverse[:, None] * inner,
        jnp.sum(cotangent * scaled, axis=0),
        jnp.sum(cotangent, axis=0),
    )


def visible_rows(token_ids, seq_rows):
    length = token_ids.shape[0]
    memory_rows = (seq_rows - length) // 2
    row_ids = jnp.concatenate(
        [
            jnp.full((memory_rows,), -1, jnp.int32),
            token_ids,
            jnp.full((memory_rows,), length, jnp.int32),
        ]
    )
    return row_ids[None, :] <= row_ids[:, None]


def masked_scores(queries, key_rows, token_ids):
    inv_root = queries.shape[-1] ** (-0.5)
    scores = (
        jnp.einsum("qhe,khe->hqk", queries, key_rows, preferred_element_type=jnp.float32) * inv_root
    )
    visible = visible_rows(token_ids, queries.shape[0])
    return jnp.where(visible[None], scores, NEGATIVE)


def attend(packed):
    queries, key_rows, values, token_ids = packed
    masked = masked_scores(queries, key_rows, token_ids)
    highest = jnp.max(masked, axis=-1, keepdims=True)
    exponent = jnp.exp(masked - highest)
    summed = jnp.sum(exponent, axis=-1, keepdims=True)
    attn_weights = (exponent / summed).astype(jnp.bfloat16)
    mixed_out = jnp.einsum("hqk,khe->qhe", attn_weights, values, preferred_element_type=jnp.float32)
    return (mixed_out.astype(jnp.bfloat16), (highest + jnp.log(summed))[..., 0])


def attend_back(packed):
    queries, key_rows, values, token_ids, log_totals, grad_mixed = packed
    inv_root = queries.shape[-1] ** (-0.5)
    masked = masked_scores(queries, key_rows, token_ids)
    probs_full = jnp.exp(masked - log_totals[..., None])
    attn_weights = probs_full.astype(jnp.bfloat16)
    grad_probs = jnp.einsum("qhe,khe->hqk", grad_mixed, values, preferred_element_type=jnp.float32)
    row_inner = jnp.sum(probs_full * grad_probs, axis=-1, keepdims=True)
    grad_scores = (probs_full * (grad_probs - row_inner)).astype(jnp.bfloat16)
    grad_queries = (
        jnp.einsum("hqk,khe->qhe", grad_scores, key_rows, preferred_element_type=jnp.float32)
        * inv_root
    )
    grad_keys = (
        jnp.einsum("hqk,qhe->khe", grad_scores, queries, preferred_element_type=jnp.float32)
        * inv_root
    )
    grad_values = jnp.einsum(
        "hqk,qhe->khe", attn_weights, grad_mixed, preferred_element_type=jnp.float32
    )
    return (
        grad_queries.astype(jnp.bfloat16),
        grad_keys.astype(jnp.bfloat16),
        grad_values.astype(jnp.bfloat16),
    )


def per_device(
    tokens,
    memory,
    block_ids,
    valid,
    teacher,
    w_qkv,
    bias_qv,
    w_out,
    bias_out,
    ln1_gain,
    ln1_bias,
    w_up,
    bias_up,
    w_down,
    bias_down,
    ln2_gain,
    ln2_bias,
):
    seq_count, feat_cols, length = tokens.shape
    memory_rows = memory.shape[1] // 2
    seq_rows = length + 2 * memory_rows
    row_count = seq_count * seq_rows
    row_size = lax.axis_size("row")
    col_size = lax.axis_size("col")
    row_place = lax.axis_index("row")
    col_place = lax.axis_index("col")
    head_rows = w_qkv.shape[0]
    head_size = bias_qv.shape[1] // 2
    feat_total = feat_cols * col_size
    head_local = head_rows * row_size // col_size
    unit_total = bias_up.shape[0] * row_size
    unit_local = unit_total // col_size
    qkv_blocks = w_qkv.reshape(head_rows, feat_cols, 3 * head_size)
    up_blocks = jnp.transpose(w_up)
    down_blocks = jnp.transpose(w_down)
    whole = (
        lax.all_gather(qkv_blocks[None], ("row", "col"), axis=0, tiled=True),
        lax.all_gather(w_out[None], ("row", "col"), axis=0, tiled=True),
        lax.all_gather(up_blocks[None], ("row", "col"), axis=0, tiled=True),
        lax.all_gather(down_blocks[None], ("row", "col"), axis=0, tiled=True),
    )
    full_qkv = assemble(whole[0], row_size, col_size)
    full_out = assemble(whole[1], row_size, col_size)
    full_up = assemble(whole[2], row_size, col_size)
    full_down = assemble(whole[3], row_size, col_size)
    qkv_heads = lax.dynamic_slice_in_dim(full_qkv, col_place * head_local, head_local, 0)
    out_rows = lax.dynamic_slice_in_dim(
        full_out, col_place * (head_local * head_size), head_local * head_size, 0
    )
    up_rows = lax.dynamic_slice_in_dim(full_up, col_place * unit_local, unit_local, 0)
    down_rows = lax.dynamic_slice_in_dim(full_down, col_place * unit_local, unit_local, 0)
    bias_heads_all, bias_units_all = (
        lax.all_gather(bias_qv, "row", axis=0, tiled=True),
        lax.all_gather(bias_up, "row", axis=0, tiled=True),
    )
    bias_heads = lax.dynamic_slice_in_dim(bias_heads_all, col_place * head_local, head_local, 0)
    bias_units = lax.dynamic_slice_in_dim(bias_units_all, col_place * unit_local, unit_local, 0)
    flat_qkv = jnp.transpose(qkv_heads, (1, 0, 2)).reshape(feat_total, head_local * 3 * head_size)
    token_rows = jnp.swapaxes(tokens, 1, 2)
    inputs = jnp.concatenate(
        [memory[:, :memory_rows], token_rows, memory[:, memory_rows:]], axis=1
    ).reshape(row_count, feat_cols)
    full_in = gather_feats(inputs)
    projected = jnp.dot(full_in, flat_qkv, preferred_element_type=jnp.float32).reshape(
        seq_count, seq_rows, head_local, 3 * head_size
    )
    queries = (projected[..., :head_size] + bias_heads[:, :head_size]).astype(jnp.bfloat16)
    key_rows = projected[..., head_size : 2 * head_size].astype(jnp.bfloat16)
    values = (projected[..., 2 * head_size :] + bias_heads[:, head_size:]).astype(jnp.bfloat16)
    mixed_out, log_totals = lax.map(attend, (queries, key_rows, values, block_ids))
    mixed_rows = mixed_out.reshape(row_count, head_local * head_size)
    attn_out = (
        forward_reduce(jnp.dot(mixed_rows, out_rows, preferred_element_type=jnp.float32)) + bias_out
    )
    norm_one, scaled_one, inverse_one = norm_forward(
        inputs.astype(jnp.float32) + attn_out, ln1_gain, ln1_bias, feat_total
    )
    norm_low = norm_one.astype(jnp.bfloat16)
    full_norm = gather_feats(norm_low)
    gate_pre = against(full_norm, up_rows) + bias_units
    hidden = jax.nn.gelu(gate_pre, approximate=False).astype(jnp.bfloat16)
    branch = (
        forward_reduce(jnp.dot(hidden, down_rows, preferred_element_type=jnp.float32)) + bias_down
    )
    output_rows, scaled_two, inverse_two = norm_forward(
        norm_one + branch, ln2_gain, ln2_bias, feat_total
    )
    output_seq = output_rows.reshape(seq_count, seq_rows, feat_cols)
    offset = lax.axis_index(("dp", "row")) * seq_count
    counts = lax.dynamic_slice_in_dim(valid, offset, seq_count, 0)
    loss_scale = valid.shape[0] * length / jnp.sum(valid).astype(jnp.float32)
    kept_rows = (jnp.arange(length, dtype=jnp.int32)[None, :] < counts[:, None])[..., None]
    mismatch = output_seq[:, memory_rows : memory_rows + length] - jnp.swapaxes(
        teacher, 1, 2
    ).astype(jnp.float32)
    grad_tok = jnp.where(kept_rows, loss_scale * mismatch, 0.0)
    grad_out = jnp.pad(grad_tok, ((0, 0), (memory_rows, memory_rows), (0, 0))).reshape(
        row_count, feat_cols
    )
    grad_two, gain_two, shift_two = norm_backward(
        grad_out, scaled_two, inverse_two, ln2_gain, feat_total
    )
    grad_branch = grad_two.astype(jnp.bfloat16)
    full_branch = back_gather(grad_branch)
    grad_down_rows = outer_sum(hidden, full_branch)
    grad_bias_down = column_total(grad_branch)
    grad_hidden = against(full_branch, down_rows)
    gelu_pull = jax.vjp(partial(jax.nn.gelu, approximate=False), gate_pre)[1]
    grad_gate = gelu_pull(grad_hidden)[0].astype(jnp.bfloat16)
    grad_up_rows = outer_sum(grad_gate, full_norm)
    grad_bias_units = column_total(grad_gate)
    grad_first = grad_two + backward_reduce(
        jnp.dot(grad_gate, up_rows, preferred_element_type=jnp.float32)
    )
    grad_one, gain_one, shift_one = norm_backward(
        grad_first, scaled_one, inverse_one, ln1_gain, feat_total
    )
    grad_attn = grad_one.astype(jnp.bfloat16)
    full_attn = back_gather(grad_attn)
    grad_out_rows = outer_sum(mixed_rows, full_attn)
    grad_bias_out = column_total(grad_attn)
    grad_mixed = against(full_attn, out_rows).astype(jnp.bfloat16)
    grad_mixed = grad_mixed.reshape(seq_count, seq_rows, head_local, head_size)
    grad_queries, grad_keys, grad_values = lax.map(
        attend_back, (queries, key_rows, values, block_ids, log_totals, grad_mixed)
    )
    grad_proj = jnp.concatenate([grad_queries, grad_keys, grad_values], axis=-1).reshape(
        row_count, head_local * 3 * head_size
    )
    grad_flat = outer_sum(full_in, grad_proj).reshape(feat_total, head_local, 3 * head_size)
    grad_heads = jnp.transpose(grad_flat, (1, 0, 2))
    proj_total = column_total(grad_proj).reshape(head_local, 3 * head_size)
    grad_bias_heads = jnp.concatenate(
        [proj_total[:, :head_size], proj_total[:, 2 * head_size :]], axis=1
    )
    grad_in = grad_one + backward_reduce(against(grad_proj, flat_qkv))
    relayed = (
        lax.all_to_all(
            grad_heads.astype(jnp.bfloat16), "col", split_axis=1, concat_axis=0, tiled=True
        ).astype(grad_heads.dtype),
        lax.all_to_all(
            grad_out_rows.astype(jnp.bfloat16), "col", split_axis=1, concat_axis=0, tiled=True
        ).astype(grad_out_rows.dtype),
        lax.all_to_all(
            grad_up_rows.astype(jnp.bfloat16), "col", split_axis=1, concat_axis=0, tiled=True
        ).astype(grad_up_rows.dtype),
        lax.all_to_all(
            grad_down_rows.astype(jnp.bfloat16), "col", split_axis=1, concat_axis=0, tiled=True
        ).astype(grad_down_rows.dtype),
    )
    grid_parts = (
        lax.psum_scatter(
            relayed[0].astype(jnp.bfloat16), "row", scatter_dimension=0, tiled=True
        ).astype(jnp.float32),
        lax.psum_scatter(
            relayed[1].astype(jnp.bfloat16), "row", scatter_dimension=0, tiled=True
        ).astype(jnp.float32),
        lax.psum_scatter(
            relayed[2].astype(jnp.bfloat16), "row", scatter_dimension=0, tiled=True
        ).astype(jnp.float32),
        lax.psum_scatter(
            relayed[3].astype(jnp.bfloat16), "row", scatter_dimension=0, tiled=True
        ).astype(jnp.float32),
    )
    weight_totals = (
        lax.psum(grid_parts[0].astype(jnp.bfloat16), "dp").astype(jnp.float32),
        lax.psum(grid_parts[1].astype(jnp.bfloat16), "dp").astype(jnp.float32),
        lax.psum(grid_parts[2].astype(jnp.bfloat16), "dp").astype(jnp.float32),
        lax.psum(grid_parts[3].astype(jnp.bfloat16), "dp").astype(jnp.float32),
    )
    grad_w_qkv = weight_totals[0].reshape(head_rows, feat_cols * 3 * head_size)
    grad_w_out = weight_totals[1]
    grad_w_up = jnp.transpose(weight_totals[2])
    grad_w_down = jnp.transpose(weight_totals[3])
    heads_pad = lax.dynamic_update_slice_in_dim(
        jnp.zeros((head_local * col_size, 2 * head_size), jnp.float32),
        grad_bias_heads,
        col_place * head_local,
        0,
    )
    units_pad = lax.dynamic_update_slice_in_dim(
        jnp.zeros((unit_total,), jnp.float32), grad_bias_units, col_place * unit_local, 0
    )
    feat_stack = jnp.stack(
        [gain_one, shift_one, gain_two, shift_two, grad_bias_out, grad_bias_down]
    )
    feat_pad = lax.dynamic_update_slice_in_dim(
        jnp.zeros((6, feat_total), jnp.float32), feat_stack, col_place * feat_cols, 1
    )
    small_totals = lax.psum((heads_pad, units_pad, feat_pad), ("dp", "row", "col"))
    grad_bias_qv = lax.dynamic_slice_in_dim(small_totals[0], row_place * head_rows, head_rows, 0)
    grad_bias_up = lax.dynamic_slice_in_dim(
        small_totals[1], row_place * bias_up.shape[0], bias_up.shape[0], 0
    )
    feat_totals = lax.dynamic_slice_in_dim(small_totals[2], col_place * feat_cols, feat_cols, 1)
    grad_seq = grad_in.reshape(seq_count, seq_rows, feat_cols)
    grad_tokens = grad_seq[:, memory_rows : memory_rows + length]
    grad_memory = jnp.concatenate(
        [grad_seq[:, :memory_rows], grad_seq[:, memory_rows + length :]], axis=1
    )
    return (
        output_seq.astype(jnp.bfloat16),
        grad_tokens,
        grad_memory,
        grad_w_qkv,
        grad_bias_qv,
        grad_w_out,
        feat_totals[4],
        feat_totals[0],
        feat_totals[1],
        grad_w_up,
        grad_bias_up,
        grad_w_down,
        feat_totals[5],
        feat_totals[2],
        feat_totals[3],
    )


def solution(mesh):
    in_specs = (
        P(("dp", "row"), "col", None),
        P(("dp", "row"), None, "col"),
        P(("dp", "row"), None),
        P(),
        P(("dp", "row"), "col", None),
        P("row", "col"),
        P("row", None),
        P("row", "col"),
        P("col"),
        P("col"),
        P("col"),
        P("col", "row"),
        P("row"),
        P("col", "row"),
        P("col"),
        P("col"),
        P("col"),
    )
    out_specs = (
        P(("dp", "row"), None, "col"),
        P(("dp", "row"), None, "col"),
        P(("dp", "row"), None, "col"),
        P("row", "col"),
        P("row", None),
        P("row", "col"),
        P("col"),
        P("col"),
        P("col"),
        P("col", "row"),
        P("row"),
        P("col", "row"),
        P("col"),
        P("col"),
        P("col"),
    )
    return jax.shard_map(
        per_device, mesh=mesh, in_specs=in_specs, out_specs=out_specs, check_vma=False
    )
```

profile of v0, /device:TPU:0, one launch (start us, length us, event | category | flops | bytes accessed | tf_op | source)
XLA Modules:
  0.0 976.6 jit_solution(16924794278916850676)
XLA Ops:
  14.5 13.6 %all-gather.3 = f32[4,3,128]{2,1,0:T(4,128)S(1)} all-gather(f32[1,3,128]{2,1,0:T(4,128)S(1)} %bitcast.266), channel_id=1, replica_groups=mesh['dp'=2,'row'=4,'col'=4] {'row'}, dimensions={0}, use_global_device_ids=true | all-gather | bytes 7680 | tf_op jit(solution)/shard_map/all_gather | solution.py:191
  28.2 24.4 %all-gather.24.cloned.1.call-done = bf16[3072,192]{1,0:T(8,128)(2,1)} async-done(((bf16[192,192]{1,0:T(8,128)(2,1)}), bf16[3072,192]{1,0:T(8,128)(2,1)}) %all-gather.24.cloned.1.call-update) | async-done | bytes 1179664 | tf_op jit(solution)/shard_map/all_gather | solution.py:176
  57.5 25.1 %all-gather.14.cloned.1.call-done = bf16[2088,768]{0,1:T(8,128)(2,1)} async-done(((bf16[2088,192]{0,1:T(8,128)(2,1)}), bf16[2088,768]{0,1:T(8,128)(2,1)}) %all-gather.14.cloned.1.call-update) | async-done | bytes 3207184 | tf_op jit(solution)/shard_map/all_gather | solution.py:12
  82.5 8.7 reshape.275
  91.2 47.3 %all-gather.16.cloned.1.call-done = bf16[16,3,192,192]{3,2,1,0:T(8,128)(2,1)} async-done(((bf16[1,3,192,192]{3,2,1,0:T(8,128)(2,1)}), bf16[16,3,192,192]{3,2,1,0:T(8,128)(2,1)}) %all-gather.16.cloned.1.call-update) | async-done | bytes 3538960 | tf_op jit(solution)/shard_map/all_gather | solution.py:175
  138.5 9.7 copy.108
  148.2 7.7 reshape.238
  161.4 51.5 %while.26 = (s32[]{:T(128)}, bf16[2,1044,3,64]{1,3,2,0:T(8,128)(2,1)S(1)}, f32[2,3,1044]{2,1,0:T(4,128)}, bf16[2,1044,3,64]{1,3,2,0:T(8,128)(2,1)S(1)}, s32[2,10...) while((s32[]{:T(128)}, ...), condition=%wide.region_3.4_spmd, body=%wide.region_0.3_spmd.sunk | while | flops 864516608 | bytes 43690424 | solution.py:208
  163.9 8.0 fusion.151
  171.9 7.1 fusion.152
  179.0 7.8 fusion.153
  189.4 8.0 fusion.151
  197.4 7.1 fusion.152
  204.5 7.8 fusion.153
  223.5 36.4 %reduce-scatter.9.cloned.1.call-done = bf16[2088,192]{0,1:T(8,128)(2,1)} async-done(((bf16[2088,768]{0,1:T(8,128)(2,1)}), bf16[2088,192]{0,1:T(8,128)(2,1)}) %reduce-scatter.9.cloned.1.call-update) | async-done | bytes 801808 | tf_op jit(solution)/shard_map/reduce_scatter | solution.py:20
  261.6 10.3 %all-reduce.5 = (f32[2088]{0:T(1024)S(1)}, f32[2088]{0:T(1024)S(1)}) all-reduce(f32[2088]{0:T(1024)S(1)} %get-tuple-element.158, f32[2088]{0:T(1024)S(1)} %get-tuple-element.157), channel_id=1, replica_groups=mesh['dp'=2,'row'=4,'col'=4] {'col'}, use_global_device_ids=true, to_apply=%region_8.9 | all-reduce | flops 4176 | bytes 33408 | tf_op jit(solution)/shard_map/psum | solution.py:56
  274.6 13.3 %all-gather.4 = f32[4,1,768]{2,1,0:T(1,128)S(1)} all-gather(f32[1,1,768]{2,1,0:T(1,128)S(1)} %reshape.262), channel_id=1, replica_groups=mesh['dp'=2,'row'=4,'col'=4] {'row'}, dimensions={0}, use_global_device_ids=true | all-gather | bytes 15360 | tf_op jit(solution)/shard_map/all_gather | solution.py:192
  288.0 27.5 %all-gather.26.cloned.1.call-done = bf16[12288,192]{0,1:T(8,128)(2,1)} async-done(((bf16[768,192]{0,1:T(8,128)(2,1)}), bf16[12288,192]{0,1:T(8,128)(2,1)}) %all-gather.26.cloned.1.call-update) | async-done | bytes 4718608 | tf_op jit(solution)/shard_map/all_gather | solution.py:177
  315.5 8.2 reshape.243
  331.2 38.2 %all-gather.28.cloned.1.call-done = bf16[12288,192]{0,1:T(8,128)(2,1)} async-done(((bf16[768,192]{0,1:T(8,128)(2,1)}), bf16[12288,192]{0,1:T(8,128)(2,1)}) %all-gather.28.cloned.1.call-update) | async-done | bytes 4718608 | tf_op jit(solution)/shard_map/all_gather | solution.py:178
  369.4 8.3 reshape.245
  385.5 14.0 %all-gather.18.cloned.1.call-done = bf16[2088,768]{0,1:T(8,128)(2,1)} async-done(((bf16[2088,192]{0,1:T(8,128)(2,1)}), bf16[2088,768]{0,1:T(8,128)(2,1)}) %all-gather.18.cloned.1.call-update) | async-done | bytes 3207184 | tf_op jit(solution)/shard_map/all_gather | solution.py:12
  399.5 20.0 %multiply_convert_fusion.1 = (bf16[2088,768]{1,0:T(8,128)(2,1)S(1)}, f32[2088,768]{1,0:T(8,128)}, f32[2088,768]{1,0:T(8,128)}) fusion(f32[768]{0:T(1024)S(1)} %dynamic_slice.67, bf16[2088,768]{0,1:T(8,128)(2,1)} %all-gather.18.cloned.1.call-done, bf16[3072,768]{0,1:T(8,128)(2,1)} %bitcast.237, s32[]{:T(128)S(6)} %select_n.38), kind=kOutput, calls=%fused_computation.65 | convolution fusion | flops 2568941568 | bytes 20560900 | tf_op jit(solution)/shard_map/dot_general | solution.py:32
  421.2 5.9 convolution_convert_fusion.2
  429.2 37.2 %reduce-scatter.11.cloned.1.call-done = bf16[2088,192]{0,1:T(8,128)(2,1)} async-done(((bf16[2088,768]{0,1:T(8,128)(2,1)}), bf16[2088,192]{0,1:T(8,128)(2,1)}) %reduce-scatter.11.cloned.1.call-update) | async-done | bytes 801808 | tf_op jit(solution)/shard_map/reduce_scatter | solution.py:20
  468.7 10.6 %all-reduce.4 = (f32[2088]{0:T(1024)S(1)}, f32[2088]{0:T(1024)S(1)}) all-reduce(f32[2088]{0:T(1024)S(1)} %get-tuple-element.161, f32[2088]{0:T(1024)S(1)} %get-tuple-element.160), channel_id=1, replica_groups=mesh['dp'=2,'row'=4,'col'=4] {'col'}, use_global_device_ids=true, to_apply=%region_13.14 | all-reduce | flops 4176 | bytes 33408 | tf_op jit(solution)/shard_map/psum | solution.py:56
  500.5 10.3 %all-reduce.3 = (f32[2088]{0:T(1024)S(1)}, f32[2088]{0:T(1024)S(1)}) all-reduce(f32[2088]{0:T(1024)S(1)} %get-tuple-element.155, f32[2088]{0:T(1024)S(1)} %reduce_sum.143), channel_id=1, replica_groups=mesh['dp'=2,'row'=4,'col'=4] {'col'}, use_global_device_ids=true, to_apply=%region_18.19 | all-reduce | flops 4176 | bytes 33408 | tf_op jit(solution)/shard_map/psum | solution.py:67
  514.1 29.9 %all-gather.20.cloned.1.call-done = bf16[2088,768]{0,1:T(8,128)(2,1)} async-done(((bf16[2088,192]{0,1:T(8,128)(2,1)}), bf16[2088,768]{0,1:T(8,128)(2,1)}) %all-gather.20.cloned.1.call-update) | async-done | bytes 3207184 | tf_op jit(solution)/shard_map/all_gather | solution.py:16
  544.0 10.5 %add_convert_fusion = bf16[2088,768]{1,0:T(8,128)(2,1)S(1)} fusion(f32[2088,768]{1,0:T(8,128)} %get-tuple-element.216, f32[2088,768]{1,0:T(8,128)} %get-tuple-element.241, bf16[2088,768]{0,1:T(8,128)(2,1)} %all-gather.20.cloned.1.call-done, bf16[3072,768]{0,1:T(8,128)(2,1)} %bitcast.240, s32[]{:T(128)S(6)} %select_n.38), kind=kOutput, calls=%fused_computation.64 | convolution fusion | flops 2485555200 | bytes 20557828 | tf_op jit(solution)/shard_map/dot_general | solution.py:32
  556.2 6.0 convolution_convert_fusion.1
  562.3 39.2 %reduce-scatter.13.cloned.1.call-done = bf16[2088,192]{0,1:T(8,128)(2,1)} async-done(((bf16[2088,768]{0,1:T(8,128)(2,1)}), bf16[2088,192]{0,1:T(8,128)(2,1)}) %reduce-scatter.13.cloned.1.call-update) | async-done | bytes 801808 | tf_op jit(solution)/shard_map/reduce_scatter | solution.py:26
  606.5 10.3 %all-reduce.2 = (f32[2088]{0:T(1024)S(1)}, f32[2088]{0:T(1024)S(1)}) all-reduce(f32[2088]{0:T(1024)S(1)} %get-tuple-element.153, f32[2088]{0:T(1024)S(1)} %get-tuple-element.156), channel_id=1, replica_groups=mesh['dp'=2,'row'=4,'col'=4] {'col'}, use_global_device_ids=true, to_apply=%region_23.24 | all-reduce | flops 4176 | bytes 33408 | tf_op jit(solution)/shard_map/psum | solution.py:67
  620.3 30.1 %all-gather.22.cloned.1.call-done = bf16[2088,768]{0,1:T(8,128)(2,1)} async-done(((bf16[2088,192]{0,1:T(8,128)(2,1)}), bf16[2088,768]{0,1:T(8,128)(2,1)}) %all-gather.22.cloned.1.call-update) | async-done | bytes 3207184 | tf_op jit(solution)/shard_map/all_gather | solution.py:16
  660.9 68.2 %while.27 = (s32[]{:T(128)}, bf16[2,1044,3,64]{1,3,2,0:T(8,128)(2,1)}, bf16[2,1044,3,64]{1,3,2,0:T(8,128)(2,1)}, bf16[2,1044,3,64]{1,3,2,0:T(8,128)(2,1)}, bf16[...) while((s32[]{:T(128)}, ...), condition=%wide.region_26.27_spmd, body=%wide.region_24.26_spmd.sunk | while | flops 2124194560 | bytes 151329200 | solution.py:262
  665.2 8.2 multiply_reduce_fusion.10
  673.5 8.6 multiply_convert_fusion.3
  682.1 8.3 fusion.165
  699.2 8.2 multiply_reduce_fusion.10
  707.5 8.6 multiply_convert_fusion.3
  716.0 8.3 fusion.165
  742.7 22.5 %all_to_all.75 = bf16[3,768,192]{2,0,1:T(4,128)(2,1)S(1)} all-to-all(bf16[3,768,192]{2,0,1:T(4,128)(2,1)S(1)} %copy.121), channel_id=1, replica_groups=mesh['dp'=2,'row'=4,'col'=4] {'col'}, dimensions={1} | all-to-all | bytes 1769472 | tf_op jit(solution)/shard_map/all_to_all | solution.py:276
  772.4 18.5 %all_to_all.76 = bf16[768,4,192]{0,2,1:T(8,128)(2,1)S(1)} all-to-all(bf16[768,4,192]{0,2,1:T(8,128)(2,1)S(1)} %bitcast.250), channel_id=1, replica_groups=mesh['dp'=2,'row'=4,'col'=4] {'col'}, dimensions={1} | all-to-all | bytes 2359296 | tf_op jit(solution)/shard_map/all_to_all | solution.py:285
  797.1 18.4 %all_to_all.77 = bf16[768,4,192]{0,2,1:T(8,128)(2,1)S(1)} all-to-all(bf16[768,4,192]{0,2,1:T(8,128)(2,1)S(1)} %bitcast.251), channel_id=1, replica_groups=mesh['dp'=2,'row'=4,'col'=4] {'col'}, dimensions={1} | all-to-all | bytes 2359296 | tf_op jit(solution)/shard_map/all_to_all | solution.py:282
  820.7 10.6 %all_to_all.78 = bf16[192,4,192]{2,0,1:T(8,128)(2,1)} all-to-all(bf16[192,4,192]{2,0,1:T(8,128)(2,1)S(1)} %copy.124), channel_id=1, replica_groups=mesh['dp'=2,'row'=4,'col'=4] {'col'}, dimensions={1} | all-to-all | bytes 589824 | tf_op jit(solution)/shard_map/all_to_all | solution.py:279
  833.5 22.8 %reduce-scatter.21.cloned.1.call-done = bf16[768,192]{0,1:T(8,128)(2,1)} async-done(((bf16[3072,192]{0,1:T(8,128)(2,1)}), bf16[768,192]{0,1:T(8,128)(2,1)}) %reduce-scatter.21.cloned.1.call-update) | async-done | bytes 294928 | tf_op jit(solution)/shard_map/reduce_scatter | solution.py:296
  856.3 21.5 %reduce-scatter.19.cloned.1.call-done = bf16[192,192]{1,0:T(8,128)(2,1)} async-done(((bf16[768,192]{1,0:T(8,128)(2,1)}), bf16[192,192]{1,0:T(8,128)(2,1)}) %reduce-scatter.19.cloned.1.call-update) | async-done | bytes 73744 | tf_op jit(solution)/shard_map/reduce_scatter | solution.py:293
  893.4 39.6 %all-reduce.1 = (f32[12,128]{1,0:T(8,128)S(1)}, f32[6,768]{1,0:T(8,128)S(1)}, f32[3072]{0:T(1024)S(1)}) all-reduce(f32[12,128]{1,0:T(8,128)S(1)} %dynamic_update_slice.26, f32[6,768]{1,0:T(8,128)S(1)} %dynamic_update_slice.27, f32[3072]{0:T(1024)S(1)} %dynamic_update_slice.28), channel_id=1, replica_groups=mesh['dp'=2,'row'=4,'col'=4] {'dp','row','col'}, use_global_device_ids=true, to_apply=%region_30.31 | all-reduce | flops 9216 | bytes 73728 | tf_op jit(solution)/shard_map/psum | solution.py:328
  942.1 17.5 %reduce-scatter.15.cloned.1.call-done = bf16[2088,192]{0,1:T(8,128)(2,1)} async-done(((bf16[2088,768]{0,1:T(8,128)(2,1)}), bf16[2088,192]{0,1:T(8,128)(2,1)}) %reduce-scatter.15.cloned.1.call-update) | async-done | bytes 801808 | tf_op jit(solution)/shard_map/reduce_scatter | solution.py:26
  (301 shorter events, 190.2 us)
Async XLA Ops:
  7.2 45.4 %all-gather.24.cloned.1.call-start = ((), (), s32[]{:S(2)}) async-start(), calls=%async_computation.25 | async-start | bytes 1671168 | tf_op jit(solution)/shard_map/all_gather | solution.py:176
  7.9 74.6 %all-gather.14.cloned.1.call-start = ((), (), s32[]{:S(2)}) async-start(), calls=%async_computation.12 | async-start | bytes 4177920 | tf_op jit(solution)/shard_map/all_gather | solution.py:12
  13.3 125.2 %all-gather.16.cloned.1.call-start = ((), (), s32[]{:S(2)}) async-start(), calls=%async_computation.13 | async-start | bytes 5013504 | tf_op jit(solution)/shard_map/all_gather | solution.py:175
  14.4 245.5 %reduce-scatter.9.cloned.1.call-start = ((), (), s32[]{:S(2)}) async-start(), calls=%async_computation.14 | async-start | bytes 4177920 | tf_op jit(solution)/shard_map/reduce_scatter | solution.py:20
  179.0 8.4 copy-start.35
  204.5 8.4 copy-start.35
  212.9 9.1 copy-start.5
  222.0 37.9 %copy-start.1 = (bf16[2088,192]{0,1:T(8,128)(2,1)S(1)}, bf16[2088,192]{0,1:T(8,128)(2,1)}, u32[]{:S(2)}) copy-start(bf16[2088,192]{0,1:T(8,128)(2,1)} %reshape.236) | copy-start | bytes 2405380
  222.0 37.9 %copy-start.40 = (f32[192]{0:T(256)S(1)}, f32[192]{0:T(256)}, u32[]{:S(2)}) copy-start(f32[192]{0:T(256)} %param.29) | copy-start | bytes 2308
  222.1 49.8 %copy-start.43 = (f32[192]{0:T(256)S(1)}, f32[192]{0:T(256)}, u32[]{:S(2)}) copy-start(f32[192]{0:T(256)} %param.30) | copy-start | bytes 2308
  222.1 49.8 %copy-start.45 = (f32[192]{0:T(256)S(1)}, f32[192]{0:T(256)}, u32[]{:S(2)}) copy-start(f32[192]{0:T(256)} %param.31) | copy-start | bytes 2308
  222.1 52.5 %copy-start.49 = (f32[768]{0:T(1024)S(1)}, f32[768]{0:T(1024)}, u32[]{:S(2)}) copy-start(f32[768]{0:T(1024)} %param.33) | copy-start | bytes 9220
  222.1 93.4 %all-gather.26.cloned.1.call-start = ((), (), s32[]{:S(2)}) async-start(), calls=%async_computation.26 | async-start | bytes 5013504 | tf_op jit(solution)/shard_map/all_gather | solution.py:177
  222.7 146.7 %all-gather.28.cloned.1.call-start = ((), (), s32[]{:S(2)}) async-start(), calls=%async_computation.27 | async-start | bytes 5013504 | tf_op jit(solution)/shard_map/all_gather | solution.py:178
  223.3 176.3 %all-gather.18.cloned.1.call-start = ((), (), s32[]{:S(2)}) async-start(), calls=%async_computation.15 | async-start | bytes 4177920 | tf_op jit(solution)/shard_map/all_gather | solution.py:12
  271.9 345.0 %copy-start.26 = (f32[2088]{0:T(1024)}, f32[2088]{0:T(1024)S(1)}, u32[]{:S(2)}) copy-start(f32[2088]{0:T(1024)S(1)} %get-tuple-element.235) | copy-start | bytes 25060
  271.9 345.0 %copy-start.28 = (f32[2088]{0:T(1024)}, f32[2088]{0:T(1024)S(1)}, u32[]{:S(2)}) copy-start(f32[2088]{0:T(1024)S(1)} %get-tuple-element.236) | copy-start | bytes 25060
  274.6 191.9 %reduce-scatter.11.cloned.1.call-start = ((), (), s32[]{:S(2)}) async-start(), calls=%async_computation.16 | async-start | bytes 4177920 | tf_op jit(solution)/shard_map/reduce_scatter | solution.py:20
  427.1 39.3 %copy-start.8 = (bf16[2088,192]{0,1:T(8,128)(2,1)S(1)}, bf16[2088,192]{0,1:T(8,128)(2,1)}, u32[]{:S(2)}) copy-start(bf16[2088,192]{0,1:T(8,128)(2,1)} %reduce-scatter.9.cloned.1.call-done) | copy-start | bytes 2405380
  427.1 39.3 %copy-start.52 = (f32[192]{0:T(256)S(1)}, f32[192]{0:T(256)}, u32[]{:S(2)}) copy-start(f32[192]{0:T(256)} %param.35) | copy-start | bytes 2308
  427.1 52.2 %copy-start.42 = (f32[192]{0:T(256)S(1)}, f32[192]{0:T(256)}, u32[]{:S(2)}) copy-start(f32[192]{0:T(256)} %param.36) | copy-start | bytes 2308
  427.1 52.2 %copy-start.53 = (f32[192]{0:T(256)S(1)}, f32[192]{0:T(256)}, u32[]{:S(2)}) copy-start(f32[192]{0:T(256)} %param.37) | copy-start | bytes 2308
  427.2 116.8 %all-gather.20.cloned.1.call-start = ((), (), s32[]{:S(2)}) async-start(), calls=%async_computation.17 | async-start | bytes 4177920 | tf_op jit(solution)/shard_map/all_gather | solution.py:16
  513.6 87.9 %reduce-scatter.13.cloned.1.call-start = ((), (), s32[]{:S(2)}) async-start(), calls=%async_computation.18 | async-start | bytes 4177920 | tf_op jit(solution)/shard_map/reduce_scatter | solution.py:26
  562.2 88.1 %all-gather.22.cloned.1.call-start = ((), (), s32[]{:S(2)}) async-start(), calls=%async_computation.19 | async-start | bytes 4177920 | tf_op jit(solution)/shard_map/all_gather | solution.py:16
  616.8 37.3 %copy-start.36 = (f32[2088]{0:T(1024)}, f32[2088]{0:T(1024)S(1)}, u32[]{:S(2)}) copy-start(f32[2088]{0:T(1024)S(1)} %broadcast_multiply_fusion) | copy-start | bytes 25060
  616.8 37.3 %copy-start.38 = (f32[2088]{0:T(1024)}, f32[2088]{0:T(1024)S(1)}, u32[]{:S(2)}) copy-start(f32[2088]{0:T(1024)S(1)} %broadcast_multiply_fusion.1) | copy-start | bytes 25060
  620.0 211.4 %reduce-scatter.17.cloned.1.call-start = ((), (), s32[]{:S(2)}) async-start(), calls=%async_computation.21 | async-start | bytes 1474560 | tf_op jit(solution)/shard_map/reduce_scatter | solution.py:290
  673.5 8.6 copy-start.7
  707.5 8.6 copy-start.7
  716.0 8.3 copy-start.17
  766.5 67.0 %reduce-scatter.23.cloned.1.call-start = ((), (), s32[]{:S(2)}) async-start(), calls=%async_computation.24 | async-start | bytes 1474560 | tf_op jit(solution)/shard_map/reduce_scatter | solution.py:299
  772.4 19.8 %copy-start.22 = (bf16[2088,768]{1,0:T(8,128)(2,1)S(1)}, bf16[2088,768]{1,0:T(8,128)(2,1)}, u32[]{:S(2)}) copy-start(bf16[2088,768]{1,0:T(8,128)(2,1)} %copy-done.21) | copy-start | bytes 9621508
  792.2 64.2 %reduce-scatter.21.cloned.1.call-start = ((), (), s32[]{:S(2)}) async-start(), calls=%async_computation.23 | async-start | bytes 1474560 | tf_op jit(solution)/shard_map/reduce_scatter | solution.py:296
  797.1 20.1 %copy-start.13 = (bf16[2088,192]{0,1:T(8,128)(2,1)S(1)}, bf16[2088,192]{0,1:T(8,128)(2,1)}, u32[]{:S(2)}) copy-start(bf16[2088,192]{0,1:T(8,128)(2,1)} %copy-done.12) | copy-start | bytes 2405380
  816.7 61.1 %reduce-scatter.19.cloned.1.call-start = ((), (), s32[]{:S(2)}) async-start(), calls=%async_computation.22 | async-start | bytes 491520 | tf_op jit(solution)/shard_map/reduce_scatter | solution.py:293
  820.3 57.6 %copy-start.15 = (bf16[2088,576]{0,1:T(8,128)(2,1)S(1)}, bf16[2088,576]{0,1:T(8,128)(2,1)}, u32[]{:S(2)}) copy-start(bf16[2088,576]{0,1:T(8,128)(2,1)} %reshape.250) | copy-start | bytes 7216132
  831.4 103.6 %all-reduce.9.cloned.1.call-start = ((), (), s32[]{:S(2)}) async-start(), calls=%async_computation.28 | async-start | bytes 1966080 | tf_op jit(solution)/shard_map/psum | solution.py:304
  877.9 81.7 %reduce-scatter.15.cloned.1.call-start = ((), (), s32[]{:S(2)}) async-start(), calls=%async_computation.20 | async-start | bytes 4177920 | tf_op jit(solution)/shard_map/reduce_scatter | solution.py:26
  888.6 70.9 %copy-start.2 = (bf16[2088,192]{0,1:T(8,128)(2,1)S(1)}, bf16[2088,192]{0,1:T(8,128)(2,1)}, u32[]{:S(2)}) copy-start(bf16[2088,192]{0,1:T(8,128)(2,1)} %reshape.236) | copy-start | bytes 2405380
  888.6 70.9 %copy-start.9 = (bf16[2088,192]{0,1:T(8,128)(2,1)S(1)}, bf16[2088,192]{0,1:T(8,128)(2,1)}, u32[]{:S(2)}) copy-start(bf16[2088,192]{0,1:T(8,128)(2,1)} %reduce-scatter.9.cloned.1.call-done) | copy-start | bytes 2405380
  888.6 70.9 %copy-start.11 = (f32[2088,192]{0,1:T(8,128)S(1)}, f32[2088,192]{0,1:T(8,128)}, u32[]{:S(2)}) copy-start(f32[2088,192]{0,1:T(8,128)} %get-tuple-element.213) | copy-start | bytes 4810756
  888.6 70.9 %copy-start.27 = (f32[2088]{0:T(1024)S(1)}, f32[2088]{0:T(1024)}, u32[]{:S(2)}) copy-start(f32[2088]{0:T(1024)} %copy-done.26) | copy-start | bytes 25060
  888.6 70.9 %copy-start.29 = (f32[2088]{0:T(1024)S(1)}, f32[2088]{0:T(1024)}, u32[]{:S(2)}) copy-start(f32[2088]{0:T(1024)} %copy-done.28) | copy-start | bytes 25060
  888.6 70.9 %copy-start.37 = (f32[2088]{0:T(1024)S(1)}, f32[2088]{0:T(1024)}, u32[]{:S(2)}) copy-start(f32[2088]{0:T(1024)} %copy-done.36) | copy-start | bytes 25060
  888.7 70.9 %copy-start.39 = (f32[2088]{0:T(1024)S(1)}, f32[2088]{0:T(1024)}, u32[]{:S(2)}) copy-start(f32[2088]{0:T(1024)} %copy-done.38) | copy-start | bytes 25060
  888.7 70.9 %copy-start.41 = (f32[192]{0:T(256)S(1)}, f32[192]{0:T(256)}, u32[]{:S(2)}) copy-start(f32[192]{0:T(256)} %param.29) | copy-start | bytes 2308
  888.7 70.9 %copy-start.44 = (f32[192]{0:T(256)S(1)}, f32[192]{0:T(256)}, u32[]{:S(2)}) copy-start(f32[192]{0:T(256)} %param.30) | copy-start | bytes 2308
  (35 other events, 131.1 us)
Sparse Core Ops, SparseCore 0:
  10.3 42.2 all-gather.23
  54.2 28.3 all-gather.13
  85.4 53.1 all-gather.15
  222.2 37.6 reduce-scatter.8
  262.0 53.4 all-gather.25
  317.6 51.7 all-gather.27
  371.5 27.9 all-gather.17
  427.3 39.0 reduce-scatter.10
  513.7 30.2 all-gather.19
  562.3 39.1 reduce-scatter.12
  620.2 30.1 all-gather.21
  766.6 29.3 reduce-scatter.16
  798.3 27.9 reduce-scatter.22
  828.4 27.9 reduce-scatter.20
  858.5 19.3 reduce-scatter.18
  880.8 37.2 all-reduce.8
  920.5 39.0 reduce-scatter.14
where the time goes:
time: 987 us; the launch traced here: 977 us
  waiting for transfers between devices  413 us (42%)
  blocking collectives  178 us (18%)
  matrix products  162 us (16%)
  local copies, waits for them, and re-layouts  134 us (14%)
  other arithmetic  71.6 us (7%)
  between operations  15.7 us (2%)
    reduce_scatter x2, waiting for transfers between devices, forward_reduce(): lax.psum_scatter(partial_rows.astype(jnp.bfloat16), 'col', scatter_dimens...  73.6 us
    all_gather x2, waiting for transfers between devices, back_gather(): return lax.all_gather(shard, 'col', axis=1, tiled=True)  60 us
    reduce_scatter x2, waiting for transfers between devices, backward_reduce(): lax.psum_scatter(partial_rows.astype(jnp.bfloat16), 'col', scatter_dimens...  56.7 us
    all_gather x1, waiting for transfers between devices, per_device(): lax.all_gather(qkv_blocks[None], ('row', 'col'), axis=0, tiled=True)  47.3 us
    dot_general x4, matrix products, against(): lax.dot_general(piece_rows, matrix, (((1,), (1,)), ((), ())), preferred_e...  40 us
    psum x1, blocking collectives, per_device(): lax.psum((heads_pad, units_pad, feat_pad), ('dp', 'row', 'col'))  39.6 us
    all_gather x2, waiting for transfers between devices, gather_feats(): return lax.all_gather(shard, 'col', axis=1, tiled=True)  39.1 us
    all_gather x1, waiting for transfers between devices, per_device(): lax.all_gather(down_blocks[None], ('row', 'col'), axis=0, tiled=True)  38.2 us
  transfers between devices with their start and end apart: 17, of which 14 were waited for; matrix products, arithmetic and copies ran while one was open for 10% of the time, Pallas kernels for 0%

commit v1 on v0

--- a/solution.py
+++ b/solution.py
@@ -154,6 +154,18 @@
     ln2_gain,
     ln2_bias,
 ):
+
+    def arrange_slots(field_in, peer_axis):
+        return jnp.concatenate(
+            lax.all_to_all(
+                jnp.stack(jnp.split(field_in, lax.axis_size(peer_axis), axis=1)),
+                axis_name=peer_axis,
+                split_axis=0,
+                concat_axis=0,
+            ),
+            axis=0,
+        )
+
     seq_count, feat_cols, length = tokens.shape
     memory_rows = memory.shape[1] // 2
     seq_rows = length + 2 * memory_rows
@@ -273,9 +285,7 @@
     )
     grad_in = grad_one + backward_reduce(against(grad_proj, flat_qkv))
     relayed = (
-        lax.all_to_all(
-            grad_heads.astype(jnp.bfloat16), "col", split_axis=1, concat_axis=0, tiled=True
-        ).astype(grad_heads.dtype),
+        arrange_slots(grad_heads.astype(jnp.bfloat16), "col").astype(grad_heads.dtype),
         lax.all_to_all(
             grad_out_rows.astype(jnp.bfloat16), "col", split_axis=1, concat_axis=0, tiled=True
         ).astype(grad_out_rows.dtype),

time: 987 us -> 982 us (level)
  no operation moved by 1% of the time
where the time goes in v1:
time: 982 us; the launch traced here: 972 us
  waiting for transfers between devices  415 us (42%)
  blocking collectives  174 us (18%)
  matrix products  162 us (16%)
  local copies, waits for them, and re-layouts  131 us (13%)
  other arithmetic  71.8 us (7%)
  between operations  15.7 us (2%)
    reduce_scatter x2, waiting for transfers between devices, forward_reduce(): lax.psum_scatter(partial_rows.astype(jnp.bfloat16), 'col', scatter_dimens...  73.6 us
    all_gather x2, waiting for transfers between devices, back_gather(): return lax.all_gather(shard, 'col', axis=1, tiled=True)  60 us
    reduce_scatter x2, waiting for transfers between devices, backward_reduce(): lax.psum_scatter(partial_rows.astype(jnp.bfloat16), 'col', scatter_dimens...  56.7 us
    all_gather x1, waiting for transfers between devices, per_device(): lax.all_gather(qkv_blocks[None], ('row', 'col'), axis=0, tiled=True)  47.3 us
    dot_general x4, matrix products, against(): lax.dot_general(piece_rows, matrix, (((1,), (1,)), ((), ())), preferred_e...  40.1 us
    psum x1, blocking collectives, per_device(): lax.psum((heads_pad, units_pad, feat_pad), ('dp', 'row', 'col'))  39.6 us
    all_gather x2, waiting for transfers between devices, gather_feats(): return lax.all_gather(shard, 'col', axis=1, tiled=True)  39.1 us
    all_gather x1, waiting for transfers between devices, per_device(): lax.all_gather(down_blocks[None], ('row', 'col'), axis=0, tiled=True)  38.2 us
  transfers between devices with their start and end apart: 17, of which 14 were waited for; matrix products, arithmetic and copies ran while one was open for 10% of the time, Pallas kernels for 0%

profile of v1, /device:TPU:0, one launch (start us, length us, event | category | flops | bytes accessed | tf_op | source)
XLA Modules:
  0.0 971.9 jit_solution(12186899716325460008)
XLA Ops:
  14.5 13.6 %all-gather.3 = f32[4,3,128]{2,1,0:T(4,128)S(1)} all-gather(f32[1,3,128]{2,1,0:T(4,128)S(1)} %bitcast.269), channel_id=1, replica_groups=mesh['dp'=2,'row'=4,'col'=4] {'row'}, dimensions={0}, use_global_device_ids=true | all-gather | bytes 7680 | tf_op jit(solution)/shard_map/all_gather | solution.py:203
  28.2 24.4 %all-gather.24.cloned.1.call-done = bf16[3072,192]{1,0:T(8,128)(2,1)} async-done(((bf16[192,192]{1,0:T(8,128)(2,1)}), bf16[3072,192]{1,0:T(8,128)(2,1)}) %all-gather.24.cloned.1.call-update) | async-done | bytes 1179664 | tf_op jit(solution)/shard_map/all_gather | solution.py:188
  57.5 25.0 %all-gather.14.cloned.1.call-done = bf16[2088,768]{0,1:T(8,128)(2,1)} async-done(((bf16[2088,192]{0,1:T(8,128)(2,1)}), bf16[2088,768]{0,1:T(8,128)(2,1)}) %all-gather.14.cloned.1.call-update) | async-done | bytes 3207184 | tf_op jit(solution)/shard_map/all_gather | solution.py:12
  82.5 8.7 reshape.279
  91.2 47.3 %all-gather.16.cloned.1.call-done = bf16[16,3,192,192]{3,2,1,0:T(8,128)(2,1)} async-done(((bf16[1,3,192,192]{3,2,1,0:T(8,128)(2,1)}), bf16[16,3,192,192]{3,2,1,0:T(8,128)(2,1)}) %all-gather.16.cloned.1.call-update) | async-done | bytes 3538960 | tf_op jit(solution)/shard_map/all_gather | solution.py:187
  138.5 9.7 copy.109
  148.2 7.7 reshape.241
  161.5 51.5 %while.26 = (s32[]{:T(128)}, bf16[2,1044,3,64]{1,3,2,0:T(8,128)(2,1)S(1)}, f32[2,3,1044]{2,1,0:T(4,128)}, bf16[2,1044,3,64]{1,3,2,0:T(8,128)(2,1)S(1)}, s32[2,10...) while((s32[]{:T(128)}, ...), condition=%wide.region_3.4_spmd, body=%wide.region_0.3_spmd.sunk | while | flops 864516608 | bytes 43690424 | solution.py:220
  163.9 8.0 fusion.151
  171.9 7.1 fusion.152
  179.0 7.8 fusion.153
  189.5 8.0 fusion.151
  197.4 7.1 fusion.152
  204.5 7.8 fusion.153
  223.5 36.4 %reduce-scatter.9.cloned.1.call-done = bf16[2088,192]{0,1:T(8,128)(2,1)} async-done(((bf16[2088,768]{0,1:T(8,128)(2,1)}), bf16[2088,192]{0,1:T(8,128)(2,1)}) %reduce-scatter.9.cloned.1.call-update) | async-done | bytes 801808 | tf_op jit(solution)/shard_map/reduce_scatter | solution.py:20
  261.6 10.3 %all-reduce.5 = (f32[2088]{0:T(1024)S(1)}, f32[2088]{0:T(1024)S(1)}) all-reduce(f32[2088]{0:T(1024)S(1)} %get-tuple-element.158, f32[2088]{0:T(1024)S(1)} %get-tuple-element.157), channel_id=1, replica_groups=mesh['dp'=2,'row'=4,'col'=4] {'col'}, use_global_device_ids=true, to_apply=%region_8.9 | all-reduce | flops 4176 | bytes 33408 | tf_op jit(solution)/shard_map/psum | solution.py:56
  274.7 13.2 %all-gather.4 = f32[4,1,768]{2,1,0:T(1,128)S(1)} all-gather(f32[1,1,768]{2,1,0:T(1,128)S(1)} %reshape.266), channel_id=1, replica_groups=mesh['dp'=2,'row'=4,'col'=4] {'row'}, dimensions={0}, use_global_device_ids=true | all-gather | bytes 15360 | tf_op jit(solution)/shard_map/all_gather | solution.py:204
  288.0 27.6 %all-gather.26.cloned.1.call-done = bf16[12288,192]{0,1:T(8,128)(2,1)} async-done(((bf16[768,192]{0,1:T(8,128)(2,1)}), bf16[12288,192]{0,1:T(8,128)(2,1)}) %all-gather.26.cloned.1.call-update) | async-done | bytes 4718608 | tf_op jit(solution)/shard_map/all_gather | solution.py:189
  315.6 8.2 reshape.246
  331.3 38.2 %all-gather.28.cloned.1.call-done = bf16[12288,192]{0,1:T(8,128)(2,1)} async-done(((bf16[768,192]{0,1:T(8,128)(2,1)}), bf16[12288,192]{0,1:T(8,128)(2,1)}) %all-gather.28.cloned.1.call-update) | async-done | bytes 4718608 | tf_op jit(solution)/shard_map/all_gather | solution.py:190
  369.5 8.3 reshape.248
  385.6 14.0 %all-gather.18.cloned.1.call-done = bf16[2088,768]{0,1:T(8,128)(2,1)} async-done(((bf16[2088,192]{0,1:T(8,128)(2,1)}), bf16[2088,768]{0,1:T(8,128)(2,1)}) %all-gather.18.cloned.1.call-update) | async-done | bytes 3207184 | tf_op jit(solution)/shard_map/all_gather | solution.py:12
  399.6 20.0 %multiply_convert_fusion.1 = (bf16[2088,768]{1,0:T(8,128)(2,1)S(1)}, f32[2088,768]{1,0:T(8,128)}, f32[2088,768]{1,0:T(8,128)}) fusion(f32[768]{0:T(1024)S(1)} %dynamic_slice.67, bf16[2088,768]{0,1:T(8,128)(2,1)} %all-gather.18.cloned.1.call-done, bf16[3072,768]{0,1:T(8,128)(2,1)} %bitcast.240, s32[]{:T(128)S(6)} %select_n.38), kind=kOutput, calls=%fused_computation.65 | convolution fusion | flops 2568941568 | bytes 20560900 | tf_op jit(solution)/shard_map/dot_general | solution.py:32
  421.3 5.9 convolution_convert_fusion.2
  429.3 37.2 %reduce-scatter.11.cloned.1.call-done = bf16[2088,192]{0,1:T(8,128)(2,1)} async-done(((bf16[2088,768]{0,1:T(8,128)(2,1)}), bf16[2088,192]{0,1:T(8,128)(2,1)}) %reduce-scatter.11.cloned.1.call-update) | async-done | bytes 801808 | tf_op jit(solution)/shard_map/reduce_scatter | solution.py:20
  468.8 10.6 %all-reduce.4 = (f32[2088]{0:T(1024)S(1)}, f32[2088]{0:T(1024)S(1)}) all-reduce(f32[2088]{0:T(1024)S(1)} %get-tuple-element.161, f32[2088]{0:T(1024)S(1)} %get-tuple-element.160), channel_id=1, replica_groups=mesh['dp'=2,'row'=4,'col'=4] {'col'}, use_global_device_ids=true, to_apply=%region_13.14 | all-reduce | flops 4176 | bytes 33408 | tf_op jit(solution)/shard_map/psum | solution.py:56
  500.6 10.3 %all-reduce.3 = (f32[2088]{0:T(1024)S(1)}, f32[2088]{0:T(1024)S(1)}) all-reduce(f32[2088]{0:T(1024)S(1)} %get-tuple-element.155, f32[2088]{0:T(1024)S(1)} %reduce_sum.143), channel_id=1, replica_groups=mesh['dp'=2,'row'=4,'col'=4] {'col'}, use_global_device_ids=true, to_apply=%region_18.19 | all-reduce | flops 4176 | bytes 33408 | tf_op jit(solution)/shard_map/psum | solution.py:67
  514.2 29.9 %all-gather.20.cloned.1.call-done = bf16[2088,768]{0,1:T(8,128)(2,1)} async-done(((bf16[2088,192]{0,1:T(8,128)(2,1)}), bf16[2088,768]{0,1:T(8,128)(2,1)}) %all-gather.20.cloned.1.call-update) | async-done | bytes 3207184 | tf_op jit(solution)/shard_map/all_gather | solution.py:16
  544.1 10.5 %add_convert_fusion = bf16[2088,768]{1,0:T(8,128)(2,1)S(1)} fusion(f32[2088,768]{1,0:T(8,128)} %get-tuple-element.216, f32[2088,768]{1,0:T(8,128)} %get-tuple-element.245, bf16[2088,768]{0,1:T(8,128)(2,1)} %all-gather.20.cloned.1.call-done, bf16[3072,768]{0,1:T(8,128)(2,1)} %bitcast.243, s32[]{:T(128)S(6)} %select_n.38), kind=kOutput, calls=%fused_computation.64 | convolution fusion | flops 2485555200 | bytes 20557828 | tf_op jit(solution)/shard_map/dot_general | solution.py:32
  556.3 6.0 convolution_convert_fusion.1
  562.3 39.2 %reduce-scatter.13.cloned.1.call-done = bf16[2088,192]{0,1:T(8,128)(2,1)} async-done(((bf16[2088,768]{0,1:T(8,128)(2,1)}), bf16[2088,192]{0,1:T(8,128)(2,1)}) %reduce-scatter.13.cloned.1.call-update) | async-done | bytes 801808 | tf_op jit(solution)/shard_map/reduce_scatter | solution.py:26
  606.6 10.3 %all-reduce.2 = (f32[2088]{0:T(1024)S(1)}, f32[2088]{0:T(1024)S(1)}) all-reduce(f32[2088]{0:T(1024)S(1)} %get-tuple-element.153, f32[2088]{0:T(1024)S(1)} %get-tuple-element.156), channel_id=1, replica_groups=mesh['dp'=2,'row'=4,'col'=4] {'col'}, use_global_device_ids=true, to_apply=%region_23.24 | all-reduce | flops 4176 | bytes 33408 | tf_op jit(solution)/shard_map/psum | solution.py:67
  620.3 30.1 %all-gather.22.cloned.1.call-done = bf16[2088,768]{0,1:T(8,128)(2,1)} async-done(((bf16[2088,192]{0,1:T(8,128)(2,1)}), bf16[2088,768]{0,1:T(8,128)(2,1)}) %all-gather.22.cloned.1.call-update) | async-done | bytes 3207184 | tf_op jit(solution)/shard_map/all_gather | solution.py:16
  661.0 67.8 %while.27 = (s32[]{:T(128)}, bf16[2,1044,3,64]{1,3,2,0:T(8,128)(2,1)}, bf16[2,1044,3,64]{1,3,2,0:T(8,128)(2,1)}, bf16[2,1044,3,64]{1,3,2,0:T(8,128)(2,1)}, bf16[...) while((s32[]{:T(128)}, ...), condition=%wide.region_26.27_spmd, body=%wide.region_24.26_spmd.sunk | while | flops 2124194560 | bytes 151329200 | solution.py:274
  665.3 8.0 multiply_reduce_fusion.10
  673.4 8.6 multiply_convert_fusion.3
  681.9 8.3 fusion.165
  699.1 8.0 multiply_reduce_fusion.10
  707.2 8.6 multiply_convert_fusion.3
  715.7 8.3 fusion.165
  742.0 19.1 %all_to_all.62 = bf16[4,3,192,192]{2,3,1,0:T(8,128)(2,1)} all-to-all(bf16[4,3,192,192]{2,3,1,0:T(8,128)(2,1)S(1)} %pad_maximum_fusion.1), channel_id=1, replica_groups=mesh['dp'=2,'row'=4,'col'=4] {'col'}, dimensions={0} | all-to-all | bytes 1769472 | tf_op jit(solution)/shard_map/all_to_all | solution.py:160
  766.1 18.5 %all_to_all.63 = bf16[768,4,192]{0,2,1:T(8,128)(2,1)S(1)} all-to-all(bf16[768,4,192]{0,2,1:T(8,128)(2,1)S(1)} %bitcast.253), channel_id=1, replica_groups=mesh['dp'=2,'row'=4,'col'=4] {'col'}, dimensions={1} | all-to-all | bytes 2359296 | tf_op jit(solution)/shard_map/all_to_all | solution.py:295
  790.7 18.4 %all_to_all.64 = bf16[768,4,192]{0,2,1:T(8,128)(2,1)S(1)} all-to-all(bf16[768,4,192]{0,2,1:T(8,128)(2,1)S(1)} %bitcast.254), channel_id=1, replica_groups=mesh['dp'=2,'row'=4,'col'=4] {'col'}, dimensions={1} | all-to-all | bytes 2359296 | tf_op jit(solution)/shard_map/all_to_all | solution.py:292
  814.3 10.6 %all_to_all.65 = bf16[192,4,192]{2,0,1:T(8,128)(2,1)} all-to-all(bf16[192,4,192]{2,0,1:T(8,128)(2,1)S(1)} %copy.123), channel_id=1, replica_groups=mesh['dp'=2,'row'=4,'col'=4] {'col'}, dimensions={1} | all-to-all | bytes 589824 | tf_op jit(solution)/shard_map/all_to_all | solution.py:289
  827.3 24.3 %reduce-scatter.21.cloned.1.call-done = bf16[768,192]{0,1:T(8,128)(2,1)} async-done(((bf16[3072,192]{0,1:T(8,128)(2,1)}), bf16[768,192]{0,1:T(8,128)(2,1)}) %reduce-scatter.21.cloned.1.call-update) | async-done | bytes 294928 | tf_op jit(solution)/shard_map/reduce_scatter | solution.py:306
  851.6 21.6 %reduce-scatter.19.cloned.1.call-done = bf16[192,192]{1,0:T(8,128)(2,1)} async-done(((bf16[768,192]{1,0:T(8,128)(2,1)}), bf16[192,192]{1,0:T(8,128)(2,1)}) %reduce-scatter.19.cloned.1.call-update) | async-done | bytes 73744 | tf_op jit(solution)/shard_map/reduce_scatter | solution.py:303
  888.7 39.6 %all-reduce.1 = (f32[12,128]{1,0:T(8,128)S(1)}, f32[6,768]{1,0:T(8,128)S(1)}, f32[3072]{0:T(1024)S(1)}) all-reduce(f32[12,128]{1,0:T(8,128)S(1)} %dynamic_update_slice.26, f32[6,768]{1,0:T(8,128)S(1)} %dynamic_update_slice.27, f32[3072]{0:T(1024)S(1)} %dynamic_update_slice.28), channel_id=1, replica_groups=mesh['dp'=2,'row'=4,'col'=4] {'dp','row','col'}, use_global_device_ids=true, to_apply=%region_30.31 | all-reduce | flops 9216 | bytes 73728 | tf_op jit(solution)/shard_map/psum | solution.py:338
  937.3 17.5 %reduce-scatter.15.cloned.1.call-done = bf16[2088,192]{0,1:T(8,128)(2,1)} async-done(((bf16[2088,768]{0,1:T(8,128)(2,1)}), bf16[2088,192]{0,1:T(8,128)(2,1)}) %reduce-scatter.15.cloned.1.call-update) | async-done | bytes 801808 | tf_op jit(solution)/shard_map/reduce_scatter | solution.py:26
  (302 shorter events, 187.6 us)
Async XLA Ops:
  7.2 45.4 %all-gather.24.cloned.1.call-start = ((), (), s32[]{:S(2)}) async-start(), calls=%async_computation.25 | async-start | bytes 1671168 | tf_op jit(solution)/shard_map/all_gather | solution.py:188
  7.9 74.6 %all-gather.14.cloned.1.call-start = ((), (), s32[]{:S(2)}) async-start(), calls=%async_computation.12 | async-start | bytes 4177920 | tf_op jit(solution)/shard_map/all_gather | solution.py:12
  13.3 125.2 %all-gather.16.cloned.1.call-start = ((), (), s32[]{:S(2)}) async-start(), calls=%async_computation.13 | async-start | bytes 5013504 | tf_op jit(solution)/shard_map/all_gather | solution.py:187
  14.4 245.5 %reduce-scatter.9.cloned.1.call-start = ((), (), s32[]{:S(2)}) async-start(), calls=%async_computation.14 | async-start | bytes 4177920 | tf_op jit(solution)/shard_map/reduce_scatter | solution.py:20
  179.0 8.4 copy-start.35
  204.5 8.4 copy-start.35
  213.0 9.1 copy-start.5
  222.1 37.9 %copy-start.1 = (bf16[2088,192]{0,1:T(8,128)(2,1)S(1)}, bf16[2088,192]{0,1:T(8,128)(2,1)}, u32[]{:S(2)}) copy-start(bf16[2088,192]{0,1:T(8,128)(2,1)} %reshape.239) | copy-start | bytes 2405380
  222.1 37.9 %copy-start.40 = (f32[192]{0:T(256)S(1)}, f32[192]{0:T(256)}, u32[]{:S(2)}) copy-start(f32[192]{0:T(256)} %param.29) | copy-start | bytes 2308
  222.1 49.8 %copy-start.43 = (f32[192]{0:T(256)S(1)}, f32[192]{0:T(256)}, u32[]{:S(2)}) copy-start(f32[192]{0:T(256)} %param.30) | copy-start | bytes 2308
  222.1 49.8 %copy-start.45 = (f32[192]{0:T(256)S(1)}, f32[192]{0:T(256)}, u32[]{:S(2)}) copy-start(f32[192]{0:T(256)} %param.31) | copy-start | bytes 2308
  222.1 52.5 %copy-start.49 = (f32[768]{0:T(1024)S(1)}, f32[768]{0:T(1024)}, u32[]{:S(2)}) copy-start(f32[768]{0:T(1024)} %param.33) | copy-start | bytes 9220
  222.1 93.4 %all-gather.26.cloned.1.call-start = ((), (), s32[]{:S(2)}) async-start(), calls=%async_computation.26 | async-start | bytes 5013504 | tf_op jit(solution)/shard_map/all_gather | solution.py:189
  222.7 146.7 %all-gather.28.cloned.1.call-start = ((), (), s32[]{:S(2)}) async-start(), calls=%async_computation.27 | async-start | bytes 5013504 | tf_op jit(solution)/shard_map/all_gather | solution.py:190
  223.3 176.3 %all-gather.18.cloned.1.call-start = ((), (), s32[]{:S(2)}) async-start(), calls=%async_computation.15 | async-start | bytes 4177920 | tf_op jit(solution)/shard_map/all_gather | solution.py:12
  271.9 345.0 %copy-start.26 = (f32[2088]{0:T(1024)}, f32[2088]{0:T(1024)S(1)}, u32[]{:S(2)}) copy-start(f32[2088]{0:T(1024)S(1)} %get-tuple-element.239) | copy-start | bytes 25060
  271.9 345.0 %copy-start.28 = (f32[2088]{0:T(1024)}, f32[2088]{0:T(1024)S(1)}, u32[]{:S(2)}) copy-start(f32[2088]{0:T(1024)S(1)} %get-tuple-element.240) | copy-start | bytes 25060
  274.6 191.9 %reduce-scatter.11.cloned.1.call-start = ((), (), s32[]{:S(2)}) async-start(), calls=%async_computation.16 | async-start | bytes 4177920 | tf_op jit(solution)/shard_map/reduce_scatter | solution.py:20
  427.2 39.3 %copy-start.8 = (bf16[2088,192]{0,1:T(8,128)(2,1)S(1)}, bf16[2088,192]{0,1:T(8,128)(2,1)}, u32[]{:S(2)}) copy-start(bf16[2088,192]{0,1:T(8,128)(2,1)} %reduce-scatter.9.cloned.1.call-done) | copy-start | bytes 2405380
  427.2 39.3 %copy-start.52 = (f32[192]{0:T(256)S(1)}, f32[192]{0:T(256)}, u32[]{:S(2)}) copy-start(f32[192]{0:T(256)} %param.35) | copy-start | bytes 2308
  427.2 52.2 %copy-start.42 = (f32[192]{0:T(256)S(1)}, f32[192]{0:T(256)}, u32[]{:S(2)}) copy-start(f32[192]{0:T(256)} %param.36) | copy-start | bytes 2308
  427.2 52.2 %copy-start.53 = (f32[192]{0:T(256)S(1)}, f32[192]{0:T(256)}, u32[]{:S(2)}) copy-start(f32[192]{0:T(256)} %param.37) | copy-start | bytes 2308
  427.2 116.8 %all-gather.20.cloned.1.call-start = ((), (), s32[]{:S(2)}) async-start(), calls=%async_computation.17 | async-start | bytes 4177920 | tf_op jit(solution)/shard_map/all_gather | solution.py:16
  513.6 87.9 %reduce-scatter.13.cloned.1.call-start = ((), (), s32[]{:S(2)}) async-start(), calls=%async_computation.18 | async-start | bytes 4177920 | tf_op jit(solution)/shard_map/reduce_scatter | solution.py:26
  562.3 88.1 %all-gather.22.cloned.1.call-start = ((), (), s32[]{:S(2)}) async-start(), calls=%async_computation.19 | async-start | bytes 4177920 | tf_op jit(solution)/shard_map/all_gather | solution.py:16
  616.9 37.3 %copy-start.36 = (f32[2088]{0:T(1024)}, f32[2088]{0:T(1024)S(1)}, u32[]{:S(2)}) copy-start(f32[2088]{0:T(1024)S(1)} %broadcast_multiply_fusion) | copy-start | bytes 25060
  616.9 37.3 %copy-start.38 = (f32[2088]{0:T(1024)}, f32[2088]{0:T(1024)S(1)}, u32[]{:S(2)}) copy-start(f32[2088]{0:T(1024)S(1)} %broadcast_multiply_fusion.1) | copy-start | bytes 25060
  620.1 204.9 %reduce-scatter.17.cloned.1.call-start = ((), (), s32[]{:S(2)}) async-start(), calls=%async_computation.21 | async-start | bytes 1474560 | tf_op jit(solution)/shard_map/reduce_scatter | solution.py:300
  673.4 8.6 copy-start.7
  707.2 8.6 copy-start.7
  741.7 19.5 %copy-start.54 = (bf16[2088,768]{0,1:T(8,128)(2,1)S(1)}, bf16[2088,768]{0,1:T(8,128)(2,1)}, u32[]{:S(2)}) copy-start(bf16[2088,768]{0,1:T(8,128)(2,1)} %all-gather.20.cloned.1.call-done) | copy-start | bytes 9621508
  761.2 66.1 %reduce-scatter.23.cloned.1.call-start = ((), (), s32[]{:S(2)}) async-start(), calls=%async_computation.24 | async-start | bytes 1474560 | tf_op jit(solution)/shard_map/reduce_scatter | solution.py:309
  766.1 19.8 %copy-start.22 = (bf16[2088,768]{1,0:T(8,128)(2,1)S(1)}, bf16[2088,768]{1,0:T(8,128)(2,1)}, u32[]{:S(2)}) copy-start(bf16[2088,768]{1,0:T(8,128)(2,1)} %copy-done.21) | copy-start | bytes 9621508
  785.8 65.8 %reduce-scatter.21.cloned.1.call-start = ((), (), s32[]{:S(2)}) async-start(), calls=%async_computation.23 | async-start | bytes 1474560 | tf_op jit(solution)/shard_map/reduce_scatter | solution.py:306
  790.7 20.0 %copy-start.13 = (bf16[2088,192]{0,1:T(8,128)(2,1)S(1)}, bf16[2088,192]{0,1:T(8,128)(2,1)}, u32[]{:S(2)}) copy-start(bf16[2088,192]{0,1:T(8,128)(2,1)} %copy-done.12) | copy-start | bytes 2405380
  810.3 62.8 %reduce-scatter.19.cloned.1.call-start = ((), (), s32[]{:S(2)}) async-start(), calls=%async_computation.22 | async-start | bytes 491520 | tf_op jit(solution)/shard_map/reduce_scatter | solution.py:303
  813.9 59.3 %copy-start.15 = (bf16[2088,576]{0,1:T(8,128)(2,1)S(1)}, bf16[2088,576]{0,1:T(8,128)(2,1)}, u32[]{:S(2)}) copy-start(bf16[2088,576]{0,1:T(8,128)(2,1)} %reshape.253) | copy-start | bytes 7216132
  825.0 105.2 %all-reduce.9.cloned.1.call-start = ((), (), s32[]{:S(2)}) async-start(), calls=%async_computation.28 | async-start | bytes 1966080 | tf_op jit(solution)/shard_map/psum | solution.py:314
  873.2 81.6 %reduce-scatter.15.cloned.1.call-start = ((), (), s32[]{:S(2)}) async-start(), calls=%async_computation.20 | async-start | bytes 4177920 | tf_op jit(solution)/shard_map/reduce_scatter | solution.py:26
  883.9 70.9 %copy-start.2 = (bf16[2088,192]{0,1:T(8,128)(2,1)S(1)}, bf16[2088,192]{0,1:T(8,128)(2,1)}, u32[]{:S(2)}) copy-start(bf16[2088,192]{0,1:T(8,128)(2,1)} %reshape.239) | copy-start | bytes 2405380
  883.9 70.9 %copy-start.9 = (bf16[2088,192]{0,1:T(8,128)(2,1)S(1)}, bf16[2088,192]{0,1:T(8,128)(2,1)}, u32[]{:S(2)}) copy-start(bf16[2088,192]{0,1:T(8,128)(2,1)} %reduce-scatter.9.cloned.1.call-done) | copy-start | bytes 2405380
  883.9 70.9 %copy-start.11 = (f32[2088,192]{0,1:T(8,128)S(1)}, f32[2088,192]{0,1:T(8,128)}, u32[]{:S(2)}) copy-start(f32[2088,192]{0,1:T(8,128)} %get-tuple-element.213) | copy-start | bytes 4810756
  883.9 70.9 %copy-start.27 = (f32[2088]{0:T(1024)S(1)}, f32[2088]{0:T(1024)}, u32[]{:S(2)}) copy-start(f32[2088]{0:T(1024)} %copy-done.26) | copy-start | bytes 25060
  883.9 70.9 %copy-start.29 = (f32[2088]{0:T(1024)S(1)}, f32[2088]{0:T(1024)}, u32[]{:S(2)}) copy-start(f32[2088]{0:T(1024)} %copy-done.28) | copy-start | bytes 25060
  883.9 70.9 %copy-start.37 = (f32[2088]{0:T(1024)S(1)}, f32[2088]{0:T(1024)}, u32[]{:S(2)}) copy-start(f32[2088]{0:T(1024)} %copy-done.36) | copy-start | bytes 25060
  884.0 70.9 %copy-start.39 = (f32[2088]{0:T(1024)S(1)}, f32[2088]{0:T(1024)}, u32[]{:S(2)}) copy-start(f32[2088]{0:T(1024)} %copy-done.38) | copy-start | bytes 25060
  884.0 70.9 %copy-start.41 = (f32[192]{0:T(256)S(1)}, f32[192]{0:T(256)}, u32[]{:S(2)}) copy-start(f32[192]{0:T(256)} %param.29) | copy-start | bytes 2308
  884.0 70.9 %copy-start.44 = (f32[192]{0:T(256)S(1)}, f32[192]{0:T(256)}, u32[]{:S(2)}) copy-start(f32[192]{0:T(256)} %param.30) | copy-start | bytes 2308
  (35 other events, 137.0 us)
Sparse Core Ops, SparseCore 0:
  10.3 42.2 all-gather.23
  54.2 28.3 all-gather.13
  85.4 53.1 all-gather.15
  222.3 37.6 reduce-scatter.8
  262.0 53.5 all-gather.25
  317.6 51.7 all-gather.27
  371.6 27.9 all-gather.17
  427.4 39.0 reduce-scatter.10
  513.8 30.2 all-gather.19
  562.4 39.1 reduce-scatter.12
  620.2 30.1 all-gather.21
  761.3 29.3 reduce-scatter.16
  793.0 27.9 reduce-scatter.22
  823.7 27.9 reduce-scatter.20
  853.7 19.3 reduce-scatter.18
  876.1 37.1 all-reduce.8
  915.7 39.0 reduce-scatter.14
